TPU v7x, 32 devices: a whole 2x2x4 slice. The times are simulated.
32 devices in a mesh: row: 8 (over y, x, core), col: 4 (over z).
Axes of the slice: x: 2, y: 2, z: 4, core: 2. Of those that a mesh axis runs over, the one named last changes fastest.
Arguments:
- voltage: bfloat16 [8, 4, 2048, 256], P('row', 'col'), may hold values from -6 to 6
- sources: bfloat16 [8, 4, 2048, 256], P('row', 'col'), may hold values from -6 to 6
- capacity: float32 [8, 4, 2048], P('row', 'col'), may hold values from 0.1 to 1
- inverse: bfloat16 [8, 4, 2048, 2048], P('row', 'col')
- couple: bfloat16 [8, 4, 256, 1024], P('row', 'col'), may hold values from -0.1875 to 0.1875
- boundary: int32 [8, 4, 256], P('row', 'col'), may hold values from 0 to 2047, as said below
- panels: bfloat16 [8, 4, 5, 16, 3, 128, 128], P('row', 'col'), may hold values from -0.125 to 0.125
- pattern: int32 [8, 4, 5, 16, 3], P('row', 'col'), may hold values from 0 to 15
Outputs:
- settled: float32 [8, 4, 2048, 256], P('row', 'col')
Inputs may be any that keep to these rules, and one draw needn't show every extreme that they name: `boundary`: the 256 indices of one subdomain are distinct.
All inputs are finite; a program needn't handle non-finite values.
Results may differ from a plain program's by a relative error of at most 0.007.
Values may be sent and summed in bfloat16 or wider, within the bound.
A program may use at most 128 MiB of HBM per device.

v0:
```python
import jax
import jax.numpy as jnp
from jax import lax
from jax.sharding import PartitionSpec as P

NI = 2048
BLK = 128
STEPS = 2
NB = 16


def swapped(value, axis, apart):
    mask = 2**apart
    pairs = [(source, source ^ mask) for source in range(lax.axis_size(axis))]
    return lax.ppermute(value, axis, pairs)


def merge_level(merged, received, blocks, columns):
    width = merged.shape[1]
    tiles = received.reshape(NB, BLK, width)
    picked = tiles[columns]
    update = jnp.einsum("nkij,nkjr->nir", blocks, picked, preferred_element_type=jnp.float32)
    return merged + update.reshape(NI, width)


def settle(loaded, inverse_block, panel_block, pattern_block):
    merged = jnp.dot(inverse_block, loaded, preferred_element_type=jnp.float32)
    col_levels = lax.axis_size("col").bit_length() - 1
    row_levels = lax.axis_size("row").bit_length() - 1
    for col_bit in range(col_levels):
        received = swapped(merged.astype(jnp.bfloat16), "col", col_bit)
        merged = merge_level(merged, received, panel_block[col_bit], pattern_block[col_bit])
    for row_bit in range(row_levels):
        level = col_levels + row_bit
        received = swapped(merged.astype(jnp.bfloat16), "row", row_bit)
        merged = merge_level(merged, received, panel_block[level], pattern_block[level])
    return merged


def per_device(voltage, sources, capacity, inverse, couple, boundary, panels, pattern):
    potential = voltage[0, 0].astype(jnp.float32)
    injected = sources[0, 0].astype(jnp.float32)
    cap_column = capacity[0, 0][:, None]
    inverse_block = inverse[0, 0]
    weights = couple[0, 0]
    indices = boundary[0, 0]
    panel_block = panels[0, 0]
    pattern_block = pattern[0, 0]
    for step in range(STEPS):
        edge = potential[indices].astype(jnp.bfloat16)
        coupled = jnp.dot(
            weights,
            lax.all_gather(edge, "col", axis=0, tiled=True),
            preferred_element_type=jnp.float32,
        )
        base = cap_column * potential + injected
        loaded = base.at[indices].add(coupled).astype(jnp.bfloat16)
        potential = settle(loaded, inverse_block, panel_block, pattern_block)
    return potential[None, None]


def solution(mesh):
    return jax.shard_map(
        per_device,
        mesh=mesh,
        in_specs=(
            P("row", "col", None, None),
            P("row", "col", None, None),
            P("row", "col", None),
            P("row", "col", None, None),
            P("row", "col", None, None),
            P("row", "col", None),
            P("row", "col", None, None, None, None, None),
            P("row", "col", None, None, None),
        ),
        out_specs=P("row", "col", None, None),
        check_vma=False,
    )
```

profile of v0, /device:TPU:0, one launch (start us, length us, event | category | flops | bytes accessed | tf_op | source)
XLA Modules:
  0.0 460.0 jit_solution(2226169042920708424)
XLA Ops:
  5.1 2.3 gather_fusion
  7.4 17.4 %all_gather.6 = bf16[1024,256]{1,0:T(8,128)(2,1)S(1)} all-gather(bf16[256,256]{1,0:T(8,128)(2,1)S(1)} %gather_fusion), channel_id=1, replica_groups=mesh['row'=8,'col'=4] {'col'}, dimensions={0}, use_global_device_ids=true | all-gather | bytes 655360 | tf_op jit(solution)/shard_map/all_gather | solution.py:53
  24.8 1.7 convert_add_fusion.1
  26.5 2.9 copy.44
  29.7 4.7 %scatter_fusion = f32[2048,256]{1,0:T(8,128)} fusion(f32[2048,256]{1,0:T(8,128)} %copy.44, s32[256]{0:T(256)S(1)} %bitcast.213, f32[256,256]{1,0:T(8,128)S(1)} %convolution_bitcast_fusion.1), kind=kCustom, calls=%fused_computation.12 | custom fusion | flops 65536 | bytes 787456 | tf_op jit(solution)/shard_map/scatter-add | solution.py:57
  34.4 7.7 %fusion.52 = (bf16[2048,256]{0,1:T(8,128)(2,1)S(1)}, f32[2048,256]{0,1:T(8,128)}) fusion(bf16[1,1,2048,2048]{3,2,1,0:T(8,128)(2,1)} %param.11, f32[2048,256]{1,0:T(8,128)} %scatter_fusion), kind=kOutput, calls=%fused_computation.80 | convolution fusion | flops 2148532224 | bytes 13631488 | tf_op jit(solution)/shard_map/dot_general | solution.py:27
  42.1 2.1 collective-permute-start
  44.5 21.3 %collective-permute-done = bf16[2048,256]{0,1:T(8,128)(2,1)} collective-permute-done((bf16[2048,256]{0,1:T(8,128)(2,1)S(1)}, bf16[2048,256]{0,1:T(8,128)(2,1)}, u32[]{:S(2)}, u32[]{:S(2)}) %collective-permute-start) | collective-permute-done | bytes 1048608 | tf_op jit(solution)/shard_map/ppermute | solution.py:15
  67.2 2.5 gather_fusion.1
  69.7 4.5 fusion.26
  74.2 2.9 copy.84
  77.1 4.0 fusion.51
  82.2 43.8 %collective-permute-done.1 = bf16[2048,256]{0,1:T(8,128)(2,1)} collective-permute-done((bf16[2048,256]{0,1:T(8,128)(2,1)S(1)}, bf16[2048,256]{0,1:T(8,128)(2,1)}, u32[]{:S(2)}, u32[]{:S(2)}) %collective-permute-start.1) | collective-permute-done | bytes 1048608 | tf_op jit(solution)/shard_map/ppermute | solution.py:15
  127.5 2.5 gather_fusion.2
  129.9 4.5 fusion.22
  134.4 2.9 copy.86
  137.3 4.0 fusion.50
  141.5 2.6 collective-permute-done.2
  145.6 2.5 gather_fusion.3
  148.1 4.5 fusion.18
  152.5 2.9 copy.88
  155.4 4.0 fusion.49
  161.1 23.6 %collective-permute-done.3 = bf16[2048,256]{0,1:T(8,128)(2,1)} collective-permute-done((bf16[2048,256]{0,1:T(8,128)(2,1)S(1)}, bf16[2048,256]{0,1:T(8,128)(2,1)}, u32[]{:S(2)}, u32[]{:S(2)}) %collective-permute-start.3) | collective-permute-done | bytes 1048608 | tf_op jit(solution)/shard_map/ppermute | solution.py:15
  186.2 2.5 gather_fusion.4
  188.7 4.5 fusion.14
  193.2 2.9 copy.90
  196.1 4.0 fusion.48
  201.8 22.7 %collective-permute-done.4 = bf16[2048,256]{0,1:T(8,128)(2,1)} collective-permute-done((bf16[2048,256]{0,1:T(8,128)(2,1)S(1)}, bf16[2048,256]{0,1:T(8,128)(2,1)}, u32[]{:S(2)}, u32[]{:S(2)}) %collective-permute-start.4) | collective-permute-done | bytes 1048608 | tf_op jit(solution)/shard_map/ppermute | solution.py:15
  226.0 2.5 gather_fusion.5
  228.5 4.5 fusion.10
  233.0 2.9 copy.92
  235.9 4.6 convert_add_fusion
  240.5 1.9 copy.61
  242.4 2.3 copy.60
  244.6 2.3 gather_fusion.6
  247.0 15.5 %all_gather.7 = bf16[1024,256]{1,0:T(8,128)(2,1)S(1)} all-gather(bf16[256,256]{1,0:T(8,128)(2,1)S(1)} %gather_fusion.6), channel_id=1, replica_groups=mesh['row'=8,'col'=4] {'col'}, dimensions={0}, use_global_device_ids=true | all-gather | bytes 655360 | tf_op jit(solution)/shard_map/all_gather | solution.py:53
  262.8 3.0 scatter_fusion.1
  265.8 7.1 %fusion.53 = (bf16[2048,256]{0,1:T(8,128)(2,1)S(1)}, f32[2048,256]{0,1:T(8,128)}) fusion(bf16[1,1,2048,2048]{3,2,1,0:T(8,128)(2,1)} %param.11, f32[2048,256]{1,0:T(8,128)S(1)} %scatter_fusion.1), kind=kOutput, calls=%fused_computation.81 | convolution fusion | flops 2148532224 | bytes 13631488 | tf_op jit(solution)/shard_map/dot_general | solution.py:27
  272.9 20.9 %collective-permute-done.5 = bf16[2048,256]{0,1:T(8,128)(2,1)S(1)} collective-permute-done((bf16[2048,256]{0,1:T(8,128)(2,1)S(1)}, bf16[2048,256]{0,1:T(8,128)(2,1)S(1)}, u32[]{:S(2)}, u32[]{:S(2)}) %collective-permute-start.5) | collective-permute-done | bytes 1048608 | tf_op jit(solution)/shard_map/ppermute | solution.py:15
  294.3 2.5 gather_fusion.7
  296.8 4.5 fusion.28
  301.3 1.9 copy.94
  303.2 3.2 fusion.47
  307.2 42.7 %collective-permute-done.6 = bf16[2048,256]{0,1:T(8,128)(2,1)S(1)} collective-permute-done((bf16[2048,256]{0,1:T(8,128)(2,1)S(1)}, bf16[2048,256]{0,1:T(8,128)(2,1)S(1)}, u32[]{:S(2)}, u32[]{:S(2)}) %collective-permute-start.6) | collective-permute-done | bytes 1048608 | tf_op jit(solution)/shard_map/ppermute | solution.py:15
  350.3 2.5 gather_fusion.8
  352.8 4.5 fusion.24
  357.3 3.1 copy.96
  360.4 3.2 fusion.46
  363.6 2.7 collective-permute-done.7
  366.8 2.5 gather_fusion.9
  369.3 4.5 fusion.20
  373.8 3.1 copy.98
  376.8 3.2 fusion.45
  381.5 23.7 %collective-permute-done.8 = bf16[2048,256]{0,1:T(8,128)(2,1)S(1)} collective-permute-done((bf16[2048,256]{0,1:T(8,128)(2,1)S(1)}, bf16[2048,256]{0,1:T(8,128)(2,1)S(1)}, u32[]{:S(2)}, u32[]{:S(2)}) %collective-permute-start.8) | collective-permute-done | bytes 1048608 | tf_op jit(solution)/shard_map/ppermute | solution.py:15
  405.8 2.5 gather_fusion.10
  408.3 4.5 fusion.16
  412.7 3.1 copy.100
  415.8 3.2 fusion.44
  420.6 22.8 %collective-permute-done.9 = bf16[2048,256]{0,1:T(8,128)(2,1)S(1)} collective-permute-done((bf16[2048,256]{0,1:T(8,128)(2,1)S(1)}, bf16[2048,256]{0,1:T(8,128)(2,1)S(1)}, u32[]{:S(2)}, u32[]{:S(2)}) %collective-permute-start.9) | collective-permute-done | bytes 1048608 | tf_op jit(solution)/shard_map/ppermute | solution.py:15
  443.9 2.5 gather_fusion.11
  446.4 4.5 fusion.12
  450.9 3.1 copy.102
  453.9 3.2 add_bitcast_fusion
  457.2 2.9 copy.72
  (58 shorter events, 24.2 us)
Async XLA Ops:
  0.0 29.4 %copy-start = (bf16[1,1,256,1024]{3,2,1,0:T(8,128)(2,1)S(1)}, bf16[1,1,256,1024]{3,2,1,0:T(8,128)(2,1)}, u32[]{:S(2)}) copy-start(bf16[1,1,256,1024]{3,2,1,0:T(8,128)(2,1)} %param.12) | copy-start | bytes 1572868
  3.7 21.0 %copy-start.6 = (f32[1,1,2048]{2,1,0:T(1,128)S(1)}, f32[1,1,2048]{2,1,0:T(1,128)}, u32[]{:S(2)}) copy-start(f32[1,1,2048]{2,1,0:T(1,128)} %param.10) | copy-start | bytes 24580
  34.4 9.9 %copy-start.7 = (s32[1,1,5,16,3]{3,1,4,2,0:T(1,128)S(1)}, s32[1,1,5,16,3]{3,1,4,2,0:T(1,128)}, u32[]{:S(2)}) copy-start(s32[1,1,5,16,3]{3,1,4,2,0:T(1,128)} %param.15) | copy-start | bytes 2884
  42.1 23.6 %collective-permute-start = (bf16[2048,256]{0,1:T(8,128)(2,1)S(1)}, bf16[2048,256]{0,1:T(8,128)(2,1)}, u32[]{:S(2)}, u32[]{:S(2)}) collective-permute-start(bf16[2048,256]{0,1:T(8,128)(2,1)S(1)} %get-tuple-element.28), channel_id=1, source_target_pairs={{0,1},{1,0},{2,3},{3,2},{4,5},{5,4},{6,7},{7,6},{8,9},{9,8},{10,11... | collective-permute-start | bytes 3145736 | tf_op jit(solution)/shard_map/ppermute | solution.py:15
  81.1 44.9 %collective-permute-start.1 = (bf16[2048,256]{0,1:T(8,128)(2,1)S(1)}, bf16[2048,256]{0,1:T(8,128)(2,1)}, u32[]{:S(2)}, u32[]{:S(2)}) collective-permute-start(bf16[2048,256]{0,1:T(8,128)(2,1)S(1)} %get-tuple-element.21), channel_id=1, source_target_pairs={{0,2},{1,3},{2,0},{3,1},{4,6},{5,7},{6,4},{7,5},{8,10},{9,11},{10,... | collective-permute-start | bytes 3145736 | tf_op jit(solution)/shard_map/ppermute | solution.py:15
  141.3 2.8 collective-permute-start.2
  159.4 25.3 %collective-permute-start.3 = (bf16[2048,256]{0,1:T(8,128)(2,1)S(1)}, bf16[2048,256]{0,1:T(8,128)(2,1)}, u32[]{:S(2)}, u32[]{:S(2)}) collective-permute-start(bf16[2048,256]{0,1:T(8,128)(2,1)S(1)} %get-tuple-element.17), channel_id=1, source_target_pairs={{0,8},{4,12},{8,0},{12,4},{16,24},{20,28},{24,16},{28,20},{1,9},{5... | collective-permute-start | bytes 3145736 | tf_op jit(solution)/shard_map/ppermute | solution.py:15
  200.1 24.4 %collective-permute-start.4 = (bf16[2048,256]{0,1:T(8,128)(2,1)S(1)}, bf16[2048,256]{0,1:T(8,128)(2,1)}, u32[]{:S(2)}, u32[]{:S(2)}) collective-permute-start(bf16[2048,256]{0,1:T(8,128)(2,1)S(1)} %get-tuple-element.15), channel_id=1, source_target_pairs={{0,16},{4,20},{8,24},{12,28},{16,0},{20,4},{24,8},{28,12},{1,17},{... | collective-permute-start | bytes 3145736 | tf_op jit(solution)/shard_map/ppermute | solution.py:15
  272.9 20.9 %collective-permute-start.5 = (bf16[2048,256]{0,1:T(8,128)(2,1)S(1)}, bf16[2048,256]{0,1:T(8,128)(2,1)S(1)}, u32[]{:S(2)}, u32[]{:S(2)}) collective-permute-start(bf16[2048,256]{0,1:T(8,128)(2,1)S(1)} %get-tuple-element.30), channel_id=1, source_target_pairs={{0,1},{1,0},{2,3},{3,2},{4,5},{5,4},{6,7},{7,6},{8,9},{9,8},{10,11... | collective-permute-start | bytes 3145736 | tf_op jit(solution)/shard_map/ppermute | solution.py:15
  306.4 43.4 %collective-permute-start.6 = (bf16[2048,256]{0,1:T(8,128)(2,1)S(1)}, bf16[2048,256]{0,1:T(8,128)(2,1)S(1)}, u32[]{:S(2)}, u32[]{:S(2)}) collective-permute-start(bf16[2048,256]{0,1:T(8,128)(2,1)S(1)} %get-tuple-element.11), channel_id=1, source_target_pairs={{0,2},{1,3},{2,0},{3,1},{4,6},{5,7},{6,4},{7,5},{8,10},{9,11},{10,... | collective-permute-start | bytes 3145736 | tf_op jit(solution)/shard_map/ppermute | solution.py:15
  357.3 3.1 copy-start.2
  363.6 2.7 collective-permute-start.7
  373.8 3.1 copy-start.3
  380.1 25.2 %collective-permute-start.8 = (bf16[2048,256]{0,1:T(8,128)(2,1)S(1)}, bf16[2048,256]{0,1:T(8,128)(2,1)S(1)}, u32[]{:S(2)}, u32[]{:S(2)}) collective-permute-start(bf16[2048,256]{0,1:T(8,128)(2,1)S(1)} %get-tuple-element.7), channel_id=1, source_target_pairs={{0,8},{4,12},{8,0},{12,4},{16,24},{20,28},{24,16},{28,20},{1,9},{5... | collective-permute-start | bytes 3145736 | tf_op jit(solution)/shard_map/ppermute | solution.py:15
  412.7 3.1 copy-start.4
  419.0 24.3 %collective-permute-start.9 = (bf16[2048,256]{0,1:T(8,128)(2,1)S(1)}, bf16[2048,256]{0,1:T(8,128)(2,1)S(1)}, u32[]{:S(2)}, u32[]{:S(2)}) collective-permute-start(bf16[2048,256]{0,1:T(8,128)(2,1)S(1)} %get-tuple-element.5), channel_id=1, source_target_pairs={{0,16},{4,20},{8,24},{12,28},{16,0},{20,4},{24,8},{28,12},{1,17},{... | collective-permute-start | bytes 3145736 | tf_op jit(solution)/shard_map/ppermute | solution.py:15
  450.9 3.1 copy-start.5
  453.9 6.1 %copy-start.1 = (bf16[1,1,256,1024]{3,2,1,0:T(8,128)(2,1)S(1)}, bf16[1,1,256,1024]{3,2,1,0:T(8,128)(2,1)}, u32[]{:S(2)}) copy-start(bf16[1,1,256,1024]{3,2,1,0:T(8,128)(2,1)} %param.12) | copy-start | bytes 1572868
where the time goes:
time: 461 us; the launch traced here: 460 us
  waiting for transfers between devices  227 us (49%)
  local copies, waits for them, and re-layouts  83.2 us (18%)
  matrix products  60.2 us (13%)
  other arithmetic  46.9 us (10%)
  blocking collectives  32.9 us (7%)
  starting transfers between devices  9.83 us (2%)
    ppermute x10, waiting for transfers between devices, swapped(): return lax.ppermute(value, axis, pairs)  227 us
    dot_general x10, matrix products, merge_level(): jnp.einsum('nkij,nkjr->nir', blocks, picked, preferred_element_type=jnp.f...  44.7 us
    all_gather x2, blocking collectives, per_device(): lax.all_gather(edge, 'col', axis=0, tiled=True)  32.9 us
    reshape x10, local copies, waits for them, and re-layouts, merge_level(): return merged + update.reshape(NI, width)  28.6 us
    gather x10, local copies, waits for them, and re-layouts, merge_level(): picked = tiles[columns]  24.9 us
    convert_element_type x6, other arithmetic, settle(): received = swapped(merged.astype(jnp.bfloat16), 'row', row_bit)  21.7 us
    dot_general x2, matrix products, settle(): merged = jnp.dot(inverse_block, loaded, preferred_element_type=jnp.float32)  14.8 us
    reshape x10, local copies, waits for them, and re-layouts, merge_level(): tiles = received.reshape(NB, BLK, width)  9.95 us
  transfers between devices with their start and end apart: 10, of which 10 were waited for; matrix products, arithmetic and copies ran while one was open for 0% of the time, Pallas kernels for 0%

commit v1 on v0

v1 whole, which is shorter than its diff:
```python
import functools

import jax
import jax.numpy as jnp
from jax import lax
from jax.experimental import pallas as pl
from jax.experimental.pallas import tpu as pltpu
from jax.sharding import PartitionSpec as P

STEPS = 2
CHUNKS = 2
PIECES = 4
F32 = jnp.float32
BF16 = jnp.bfloat16
MESH = pl.DeviceIdType.MESH


def plan(levels, col_levels):
    wire = [10.0 * 2**bit for bit in range(col_levels)]
    wire += [2.0] + [10.0] * (levels - col_levels - 1)
    wire = [t * 2 / CHUNKS for t in wire]
    stages = [(s, t) for s in range(STEPS) for t in range(-2, levels)]
    at = [0] * CHUNKS
    ready = [0.0] * CHUNKS
    links = {}
    now = 0.0
    order = []
    while any(at[c] < len(stages) for c in range(CHUNKS)):
        left = [c for c in range(CHUNKS) if at[c] < len(stages)]
        c = min(left, key=lambda k: (max(ready[k], now), k))
        s, t = stages[at[c]]
        at[c] += 1
        order.append((s, t, c))
        now = max(now, ready[c]) + (4.0 if t == -1 else 1.0)
        if t == levels - 1:
            ready[c] = now
        else:
            nxt = t + 1
            key = "z" if nxt < col_levels else nxt
            cost = 1.0 if t == -2 else wire[nxt]
            start = max(now, links.get(key, 0.0)) if t != -2 else now
            links[key] = start + cost
            ready[c] = start + cost + 1.5
    return order


def kernel(
    ncol, nrow, levels, nb, kb, blk, nbnd, rhs,
    cap_ref, bnd_ref, pat_ref, volt_hbm, src_hbm, inv_hbm, cpl_hbm, pan_hbm,
    out_hbm, *scratch,
):
    ni = nb * blk
    w = rhs // CHUNKS
    col_levels = ncol.bit_length() - 1
    (inv, pan, cpl, src, capb, hot, hot_t, load_sem, out_sem,
     gs_sem, gr_sem, ls_sem, lr_sem) = scratch[:13]
    rest = list(scratch[13:])
    merged = [rest.pop(0) for _ in range(CHUNKS)]
    low = [rest.pop(0) for _ in range(CHUNKS)]
    loaded = [rest.pop(0) for _ in range(CHUNKS)]
    edges = [[rest.pop(0) for _ in range(CHUNKS)] for _ in range(STEPS)]
    got = [[[rest.pop(0) for _ in range(CHUNKS)] for _ in range(levels)] for _ in range(STEPS)]

    loads = []
    for c in range(CHUNKS):
        cols = pl.ds(c * w, w)
        for p in range(nb):
            loads.append(pltpu.make_async_copy(
                volt_hbm.at[0, 0, pl.ds(p * blk, blk), cols], low[c].at[p], load_sem.at[0, c, p]))
    volt_loads = loads
    src_loads = [pltpu.make_async_copy(src_hbm.at[0, 0, :, pl.ds(c * w, w)], src.at[c], load_sem.at[1, c, 0]) for c in range(CHUNKS)]
    cpl_load = pltpu.make_async_copy(cpl_hbm.at[0, 0], cpl, load_sem.at[1, 0, 1])
    rows_each = ni // PIECES
    inv_loads = [pltpu.make_async_copy(inv_hbm.at[0, 0, pl.ds(p * rows_each, rows_each)], inv.at[pl.ds(p * rows_each, rows_each)], load_sem.at[1, 1, 1 + p]) for p in range(PIECES)]
    pan_loads = [pltpu.make_async_copy(pan_hbm.at[0, 0, l], pan.at[l], load_sem.at[1, 0, 2 + l]) for l in range(levels)]
    for one in volt_loads + [cpl_load] + src_loads + inv_loads + pan_loads:
        one.start()

    my_row = lax.axis_index("row")
    my_col = lax.axis_index("col")

    def flip(me, mask):
        return me + mask - 2 * mask * lax.rem(me // mask, 2)

    partners = []
    for l in range(levels):
        if l < col_levels:
            partners.append((my_row, flip(my_col, 2**l)))
        else:
            partners.append((flip(my_row, 2 ** (l - col_levels)), my_col))
    barrier = pltpu.get_barrier_semaphore()
    for o in range(1, ncol):
        pl.semaphore_signal(barrier, inc=1, device_id=(my_row, lax.rem(my_col + o, ncol)), device_id_type=MESH)
    for l in range(col_levels, levels):
        pl.semaphore_signal(barrier, inc=1, device_id=partners[l], device_id_type=MESH)

    bnd_row = bnd_ref[...]
    bnd_col = jnp.transpose(jnp.broadcast_to(bnd_row.astype(F32), (blk, nbnd)))
    for j in range(nb):
        rows = lax.broadcasted_iota(jnp.int32, (blk, nbnd), 0) + j * blk
        hot[pl.ds(j * blk, blk), :] = jnp.where(rows == bnd_row, 1.0, 0.0).astype(BF16)
        lanes = (lax.broadcasted_iota(jnp.int32, (nbnd, blk), 1) + j * blk).astype(F32)
        hot_t[:, pl.ds(j * blk, blk)] = jnp.where(lanes == bnd_col, 1.0, 0.0).astype(BF16)
        capb[pl.ds(j * blk, blk), :] = jnp.transpose(
            jnp.broadcast_to(cap_ref[:, pl.ds(j * blk, blk)], (blk, blk)))[:, :w]

    pl.semaphore_wait(barrier, ncol - 1 + levels - col_levels)

    def edge_copy(s, c, o):
        return pltpu.make_async_remote_copy(
            src_ref=edges[s][c].at[my_col], dst_ref=edges[s][c].at[my_col],
            send_sem=gs_sem.at[s, c, o], recv_sem=gr_sem.at[s, c, o],
            device_id=(my_row, lax.rem(my_col + o, ncol)), device_id_type=MESH)

    per = nb // PIECES

    def level_copy(s, l, c, p):
        return pltpu.make_async_remote_copy(
            src_ref=low[c].at[pl.ds(p * per, per)], dst_ref=got[s][l][c].at[pl.ds(p * per, per)],
            send_sem=ls_sem.at[s, l, c, p], recv_sem=lr_sem.at[s, l, c, p],
            device_id=partners[l], device_id_type=MESH)

    def out_copy(c, p):
        rows = pl.ds(p * rows_each, rows_each)
        return pltpu.make_async_copy(merged[c].at[rows], out_hbm.at[0, 0, rows, pl.ds(c * w, w)], out_sem.at[c, p])

    def gather_stage(s, c):
        if s == 0:
            for p in range(nb):
                volt_loads[c * nb + p].wait()
        state = low[c][...].reshape(ni, w)
        edges[s][c][my_col] = jnp.dot(hot_t[...], state, preferred_element_type=F32).astype(BF16)
        for o in range(1, ncol):
            edge_copy(s, c, o).start()

    def interior_stage(s, c):
        if s == 0:
            src_loads[c].wait()
            if c == 0:
                cpl_load.wait()
        for o in range(1, ncol):
            edge_copy(s, c, o).wait()
        coupled = jnp.dot(cpl[...], edges[s][c][...].reshape(ncol * nbnd, w), preferred_element_type=F32)
        high = coupled.astype(BF16)
        rest_part = (coupled - high.astype(F32)).astype(BF16)
        both = jnp.concatenate([high, rest_part], axis=1)

        def load_rows(p, carry):
            rows = pl.ds(pl.multiple_of(p * rows_each, rows_each), rows_each)
            spread = jnp.dot(hot[rows, :], both, preferred_element_type=F32)
            if s == 0:
                pot = low[c][pl.ds(p * per, per)].reshape(rows_each, w).astype(F32)
            else:
                pot = merged[c][rows, :]
            base = capb[rows, :] * pot + src[c, rows, :].astype(F32)
            loaded[c][rows, :] = (base + (spread[:, :w] + spread[:, w:])).astype(BF16)
            return carry

        lax.fori_loop(0, PIECES, load_rows, 0)
        if s == 0 and c == 0:
            for one in inv_loads:
                one.wait()

        def inner(p, carry):
            rows = pl.ds(pl.multiple_of(p * rows_each, rows_each), rows_each)
            value = jnp.dot(inv[rows, :], loaded[c][...], preferred_element_type=F32)
            merged[c][rows, :] = value
            low[c][pl.ds(p * per, per)] = value.astype(BF16).reshape(per, blk, w)
            level_copy(s, 0, c, p).start()
            return carry

        lax.fori_loop(0, PIECES, inner, 0)

    def merge_stage(s, l, c):
        if s == 0 and c == 0:
            pan_loads[l].wait()
        for p in range(PIECES):
            level_copy(s, l, c, p).wait()
        final = s == STEPS - 1 and l == levels - 1

        def piece(p, carry):
            for u in range(per):
                i = p * per + u
                rows = pl.ds(pl.multiple_of(i * blk, blk), blk)
                left = jnp.concatenate([pan[l, i, k] for k in range(kb)], axis=1)
                right = jnp.concatenate([got[s][l][c][pat_ref[0, 0, l, i, k]] for k in range(kb)], axis=0)
                value = merged[c][rows, :] + jnp.dot(left, right, preferred_element_type=F32)
                merged[c][rows, :] = value
                if not final:
                    low[c][i] = value.astype(BF16)
            if l < levels - 1:
                level_copy(s, l + 1, c, p).start()
            elif final:
                out_copy(c, p).start()
            return carry

        lax.fori_loop(0, PIECES, piece, 0)

    for s, t, c in plan(levels, col_levels):
        if t == -2:
            gather_stage(s, c)
        elif t == -1:
            interior_stage(s, c)
        else:
            merge_stage(s, t, c)
    for c in range(CHUNKS):
        for p in range(PIECES):
            out_copy(c, p).wait()


def per_device(mesh, voltage, sources, capacity, inverse, couple, boundary, panels, pattern):
    ncol, nrow = mesh.shape["col"], mesh.shape["row"]
    _, _, levels, nb, kb, blk, _ = panels.shape
    ni, rhs = voltage.shape[2:]
    nbnd = boundary.shape[2]
    w = rhs // CHUNKS
    sems = pltpu.SemaphoreType.DMA
    scratch = [
        pltpu.VMEM((ni, ni), BF16),
        pltpu.VMEM((levels, nb, kb, blk, blk), BF16),
        pltpu.VMEM((nbnd, ncol * nbnd), BF16),
        pltpu.VMEM((CHUNKS, ni, w), BF16),
        pltpu.VMEM((ni, w), F32),
        pltpu.VMEM((ni, nbnd), BF16),
        pltpu.VMEM((nbnd, ni), BF16),
        sems((2, CHUNKS, nb)),
        sems((CHUNKS, PIECES)),
        sems((STEPS, CHUNKS, ncol)),
        sems((STEPS, CHUNKS, ncol)),
        sems((STEPS, levels, CHUNKS, PIECES)),
        sems((STEPS, levels, CHUNKS, PIECES)),
    ]
    scratch += [pltpu.VMEM((ni, w), F32) for _ in range(CHUNKS)]
    scratch += [pltpu.VMEM((nb, blk, w), BF16) for _ in range(CHUNKS)]
    scratch += [pltpu.VMEM((ni, w), BF16) for _ in range(CHUNKS)]
    scratch += [pltpu.VMEM((ncol, nbnd, w), BF16) for _ in range(STEPS * CHUNKS)]
    scratch += [pltpu.VMEM((nb, blk, w), BF16) for _ in range(STEPS * levels * CHUNKS)]
    vmem = pl.BlockSpec(memory_space=pltpu.VMEM)
    smem = pl.BlockSpec(memory_space=pltpu.SMEM)
    hbm = pl.BlockSpec(memory_space=pl.ANY)
    return pl.pallas_call(
        functools.partial(kernel, ncol, nrow, levels, nb, kb, blk, nbnd, rhs),
        out_shape=jax.ShapeDtypeStruct((1, 1, ni, rhs), F32),
        in_specs=[vmem, vmem, smem, hbm, hbm, hbm, hbm, hbm],
        out_specs=hbm,
        scratch_shapes=scratch,
        compiler_params=pltpu.CompilerParams(
            collective_id=0, has_side_effects=True, vmem_limit_bytes=67_043_328),
    )(capacity.reshape(1, ni), boundary.reshape(1, nbnd), pattern, voltage, sources, inverse, couple, panels)


def solution(mesh):
    return jax.shard_map(
        functools.partial(per_device, mesh),
        mesh=mesh,
        in_specs=(
            P("row", "col", None, None),
            P("row", "col", None, None),
            P("row", "col", None),
            P("row", "col", None, None),
            P("row", "col", None, None),
            P("row", "col", None),
            P("row", "col", None, None, None, None, None),
            P("row", "col", None, None, None),
        ),
        out_specs=P("row", "col", None, None),
        check_vma=False,
    )
```

time: 461 us -> 224 us (0.49)
  waiting for transfers between devices: 227 us -> 0 us
  Pallas kernels: 0 us -> 220 us
  local copies, waits for them, and re-layouts: 83.2 us -> 4.46 us
  matrix products: 60.2 us -> 0 us
  other arithmetic: 46.9 us -> 0 us
  blocking collectives: 32.9 us -> 0 us
  starting transfers between devices: 9.83 us -> 0 us
    ppermute x10 -> x0, waiting for transfers between devices: 227 us -> none  [swapped(): return lax.ppermute(value, axis, pairs)]
    pallas_call x0 -> x1, Pallas kernels: none -> 220 us  [per_device(): pl.pallas_call(functools.partial(kernel, ncol, nrow, levels, nb, kb, blk,...]
    dot_general x14 -> x0, matrix products: 60.2 us -> none  [the longest x10 44.7 us: merge_level(): jnp.einsum('nkij,nkjr->nir', blocks, picked, preferred_element_type=jnp.f...]
    reshape x20 -> x0, local copies, waits for them, and re-layouts: 38.6 us -> none  [the longest x10 28.6 us: merge_level(): return merged + update.reshape(NI, width)]
    all_gather x2 -> x0, blocking collectives: 32.9 us -> none  [per_device(): lax.all_gather(edge, 'col', axis=0, tiled=True)]
    gather x12 -> x0, local copies, waits for them, and re-layouts: 29.5 us -> none  [the longest x10 24.9 us: merge_level(): picked = tiles[columns]]
    convert_element_type x8 -> x0, other arithmetic: 28.9 us -> none  [the longest x6 21.7 us: settle(): received = swapped(merged.astype(jnp.bfloat16), 'row', row_bit)]
    ppermute x10 -> x0, starting transfers between devices: 9.83 us -> none  [swapped(): return lax.ppermute(value, axis, pairs)]
  transfers between devices with their start and end apart: 10 -> 0, of which waited for: 10 -> 0; matrix products, arithmetic and copies ran while one was open for 0% -> 0% of each run, Pallas kernels for 0% -> 0%
where the time goes in v1:
time: 224 us
  Pallas kernels  220 us (98%)
  local copies, waits for them, and re-layouts  4.46 us (2%)
    pallas_call x1, Pallas kernels, per_device(): pl.pallas_call(functools.partial(kernel, ncol, nrow, levels, nb, kb, blk,...  220 us

profile of v1, /device:TPU:0, one launch (start us, length us, event | category | flops | bytes accessed | tf_op | source)
XLA Modules:
  0.0 224.0 jit_solution(3221867712341533814)
XLA Ops:
  0.0 1.4 copy.9.pat_ref
  1.4 219.5 %shard_map.82 = f32[1,1,2048,256]{3,2,1,0:T(8,128)} custom-call(f32[1,2048]{1,0:T(1,128)} %bitcast.2, s32[1,256]{1,0:T(1,128)} %bitcast.3, s32[1,1,5,16,3]{4,3,2,1,0:T(8,128)} %copy.9.pat_ref, bf16[1,1,2048,256]{3,2,1,0:T(8,128)(2,1)} %volt_hbm.1, bf16[1,1,2048,256]{3,2,1,0:T(8,128)(2,1)} %src_hbm.1, bf16[1,1,2048,2048]{3,2,1,0:T(8,128)(2,1)} %inv_hbm.1, ...), custom_call_target="tpu_custom_call" | custom-call | tf_op jit(solution)/shard_map/pallas_call | solution.py:241
  220.9 3.0 %copy.11 = f32[1,1,2048,256]{3,2,1,0:T(8,128)} copy(f32[1,1,2048,256]{3,2,1,0:T(8,128)} %shard_map.82) | data formatting | bytes 4194304

commit v2 on v1

v2 whole, which is shorter than its diff:
```python
import functools

import jax
import jax.numpy as jnp
from jax import lax
from jax.experimental import pallas as pl
from jax.experimental.pallas import tpu as pltpu
from jax.sharding import PartitionSpec as P

STEPS = 2
CHUNKS = 4
PIECES = 4
F32 = jnp.float32
BF16 = jnp.bfloat16
MESH = pl.DeviceIdType.MESH


def plan(levels, col_levels):
    wire = [10.0 * 2**bit for bit in range(col_levels)]
    wire += [1.5] + [10.0] * (levels - col_levels - 1)
    wire = [t * 2 / CHUNKS for t in wire]
    stages = [(0, t) for t in range(levels)]
    stages += [(s, t) for s in range(1, STEPS) for t in range(-2, levels)]
    at = [0] * CHUNKS
    ready = [2.0 + wire[0] * (c + 1) for c in range(CHUNKS)]
    links = {"z": 0.0}
    now = 0.0
    order = []
    while any(at[c] < len(stages) for c in range(CHUNKS)):
        left = [c for c in range(CHUNKS) if at[c] < len(stages)]
        c = min(left, key=lambda k: (max(ready[k], now), at[k], k))
        s, t = stages[at[c]]
        at[c] += 1
        order.append((s, t, c))
        now = max(now, ready[c]) + {-2: 0.6, -1: 3.0}.get(t, 1.0)
        if t == levels - 1:
            ready[c] = now
        elif t == -2:
            ready[c] = now + 3.0
        else:
            nxt = t + 1
            key = nxt
            start = max(now, links.get(key, 0.0))
            links[key] = start + wire[nxt]
            ready[c] = start + wire[nxt] + 1.5
    return order


def kernel(
    ncol, nrow, levels, nb, kb, blk, nbnd, rhs,
    cap_ref, bnd_ref, pat_ref, volt_hbm, src_hbm, inv_hbm, cpl_hbm, pan_hbm,
    out_hbm, *scratch,
):
    ni = nb * blk
    w = rhs // CHUNKS
    half = nb // 2
    hrows = ni // 2
    hb = nbnd // 2
    col_levels = ncol.bit_length() - 1
    (inv, pan, cpl, volt, src, capb, hot, hot_t, outb, loaded0, loaded, tiles, edge0, load_sem, out_sem,
     gs_sem, gr_sem, ls_sem, lr_sem) = scratch[:19]
    rest = list(scratch[19:])
    merged = [rest.pop(0) for _ in range(CHUNKS)]
    low = [rest.pop(0) for _ in range(CHUNKS)]
    edges = [[rest.pop(0) for _ in range(CHUNKS)] for _ in range(STEPS - 1)]
    got = [[[rest.pop(0) for _ in range(CHUNKS)] for _ in range(levels)] for _ in range(STEPS)]

    rows_each = hrows // PIECES
    volt_load = pltpu.make_async_copy(volt_hbm.at[0, 0], volt, load_sem.at[0])
    src_load = pltpu.make_async_copy(src_hbm.at[0, 0], src, load_sem.at[1])
    cpl_load = pltpu.make_async_copy(cpl_hbm.at[0, 0], cpl, load_sem.at[2])
    inv_load = pltpu.make_async_copy(inv_hbm.at[0, 0], inv, load_sem.at[3])
    pan_loads = [pltpu.make_async_copy(pan_hbm.at[0, 0, l], pan.at[l], load_sem.at[4 + l]) for l in range(levels)]
    for one in [volt_load, cpl_load, src_load, inv_load] + pan_loads:
        one.start()

    my_row = lax.axis_index("row")
    my_col = lax.axis_index("col")

    def flip(me, mask):
        return me + mask - 2 * mask * lax.rem(me // mask, 2)

    partners = []
    for l in range(levels):
        if l < col_levels:
            partners.append((my_row, flip(my_col, 2**l)))
        else:
            partners.append((flip(my_row, 2 ** (l - col_levels)), my_col))
    barrier = pltpu.get_barrier_semaphore()
    for o in range(1, ncol):
        pl.semaphore_signal(barrier, inc=1, device_id=(my_row, lax.rem(my_col + o, ncol)), device_id_type=MESH)
    for l in range(col_levels, levels):
        pl.semaphore_signal(barrier, inc=1, device_id=partners[l], device_id_type=MESH)

    bnd_row = bnd_ref[...]
    bnd_col = jnp.transpose(jnp.broadcast_to(bnd_row.astype(F32), (blk, nbnd)))
    for j in range(nb):
        rows = lax.broadcasted_iota(jnp.int32, (blk, nbnd), 0) + j * blk
        hot[pl.ds(j * blk, blk), :] = jnp.where(rows == bnd_row, 1.0, 0.0).astype(BF16)
        lanes = (lax.broadcasted_iota(jnp.int32, (nbnd, blk), 1) + j * blk).astype(F32)
        hot_t[:, pl.ds(j * blk, blk)] = jnp.where(lanes == bnd_col, 1.0, 0.0).astype(BF16)
        capb[pl.ds(j * blk, blk), :] = jnp.transpose(
            jnp.broadcast_to(cap_ref[:, pl.ds(j * blk, blk)], (blk, blk)))

    pl.semaphore_wait(barrier, ncol - 1 + levels - col_levels)

    def edge_copy(s, c, o):
        ref = edge0 if s == 0 else edges[s - 1][c]
        return pltpu.make_async_remote_copy(
            src_ref=ref.at[my_col], dst_ref=ref.at[my_col],
            send_sem=gs_sem.at[s, c, o], recv_sem=gr_sem.at[s, c, o],
            device_id=(my_row, lax.rem(my_col + o, ncol)), device_id_type=MESH)

    per = half // PIECES

    def level_copy(s, l, c, p):
        return pltpu.make_async_remote_copy(
            src_ref=low[c].at[pl.ds(p * per, per)], dst_ref=got[s][l][c].at[pl.ds(p * per, per)],
            send_sem=ls_sem.at[s, l, c, p], recv_sem=lr_sem.at[s, l, c, p],
            device_id=partners[l], device_id_type=MESH)

    def out_copy(g, p):
        rows = pl.ds(p * (ni // PIECES), ni // PIECES)
        return pltpu.make_async_copy(
            outb.at[g, rows], out_hbm.at[0, 0, rows, pl.ds(g * blk, blk)], out_sem.at[g, p])

    def split_parts(coupled):
        high = coupled.astype(BF16)
        return high, (coupled - high.astype(F32)).astype(BF16)

    def first_step():
        volt_load.wait()
        edge0[my_col] = jnp.dot(hot_t[...], volt[...], preferred_element_type=F32).astype(BF16)
        for o in range(1, ncol):
            edge_copy(0, 0, o).start()
        src_load.wait()
        cpl_load.wait()
        for o in range(1, ncol):
            edge_copy(0, 0, o).wait()
        coupled = jnp.dot(cpl[...], edge0[...].reshape(ncol * nbnd, rhs), preferred_element_type=F32)
        both = jnp.concatenate(split_parts(coupled), axis=0)

        def load_rows(p, carry):
            rows = pl.ds(pl.multiple_of(p * rows_each, rows_each), rows_each)
            ones = hot[rows, :]
            spread = jnp.dot(jnp.concatenate([ones, ones], axis=1), both, preferred_element_type=F32)
            cap = capb[rows, :]
            base = jnp.concatenate([cap] * (rhs // blk), axis=1) * volt[rows, :].astype(F32) + src[rows, :].astype(F32)
            loaded0[rows, :] = (base + spread).astype(BF16)
            return carry

        lax.fori_loop(0, 2 * PIECES, load_rows, 0)
        inv_load.wait()

        def inner(p, carry):
            rows = pl.ds(pl.multiple_of(p * rows_each, rows_each), rows_each)
            under = pl.ds(pl.multiple_of(p * rows_each, rows_each) + hrows, rows_each)
            top = jnp.dot(inv[rows, :], loaded0[...], preferred_element_type=F32)
            bottom = jnp.dot(inv[under, :], loaded0[...], preferred_element_type=F32)
            for c in range(CHUNKS):
                value = jnp.concatenate([top[:, c * w:(c + 1) * w], bottom[:, c * w:(c + 1) * w]], axis=1)
                merged[c][rows, :] = value
                low[c][pl.ds(p * per, per)] = value.astype(BF16).reshape(per, blk, blk)
            level_copy(0, 0, 0, p).start()
            return carry

        lax.fori_loop(0, PIECES, inner, 0)
        for c in range(1, CHUNKS):
            for p in range(PIECES):
                level_copy(0, 0, c, p).start()

    def gather_stage(s, c):
        state = low[c][...].reshape(hrows, blk)
        first = jnp.dot(hot_t[:, :hrows], state, preferred_element_type=F32)
        second = jnp.dot(hot_t[:, hrows:], state, preferred_element_type=F32)
        edge = first[:, :w] + second[:, w:]
        edges[s - 1][c][my_col] = jnp.concatenate([edge[:hb], edge[hb:]], axis=1).astype(BF16)
        for o in range(1, ncol):
            edge_copy(s, c, o).start()

    def interior_stage(s, c):
        for o in range(1, ncol):
            edge_copy(s, c, o).wait()
        parts = []
        for j in range(ncol):
            packed = edges[s - 1][c][j]
            parts += [packed[:, :w], packed[:, w:]]
        coupled = jnp.dot(cpl[...], jnp.concatenate(parts, axis=0), preferred_element_type=F32)
        both = jnp.concatenate(split_parts(coupled), axis=0)

        def load_rows(p, carry):
            for part in range(2):
                rows = pl.ds(pl.multiple_of(p * rows_each, rows_each), rows_each)
                full = pl.ds(pl.multiple_of(p * rows_each, rows_each) + part * hrows, rows_each)
                ones = hot[full, :]
                spread = jnp.dot(jnp.concatenate([ones, ones], axis=1), both, preferred_element_type=F32)
                pot = merged[c][rows, part * w:(part + 1) * w]
                given = src[full, c * w:(c + 1) * w].astype(F32)
                loaded[full, :] = (capb[full, :w] * pot + given + spread).astype(BF16)
            return carry

        lax.fori_loop(0, PIECES, load_rows, 0)

        def inner(p, carry):
            rows = pl.ds(pl.multiple_of(p * rows_each, rows_each), rows_each)
            under = pl.ds(pl.multiple_of(p * rows_each, rows_each) + hrows, rows_each)
            top = jnp.dot(inv[rows, :], loaded[...], preferred_element_type=F32)
            bottom = jnp.dot(inv[under, :], loaded[...], preferred_element_type=F32)
            value = jnp.concatenate([top, bottom], axis=1)
            merged[c][rows, :] = value
            low[c][pl.ds(p * per, per)] = value.astype(BF16).reshape(per, blk, blk)
            level_copy(s, 0, c, p).start()
            return carry

        lax.fori_loop(0, PIECES, inner, 0)

    def merge_stage(s, l, c):
        if s == 0 and c == 0:
            pan_loads[l].wait()
        for p in range(PIECES):
            level_copy(s, l, c, p).wait()
        final = s == STEPS - 1 and l == levels - 1
        for q in range(half):
            packed = got[s][l][c][q]
            tiles[q] = packed[:, :w]
            tiles[q + half] = packed[:, w:]

        def product(i):
            left = jnp.concatenate([pan[l, i, k] for k in range(kb)], axis=1)
            right = jnp.concatenate([tiles[pat_ref[0, 0, l, i, k]] for k in range(kb)], axis=0)
            return jnp.dot(left, right, preferred_element_type=F32)

        def piece(p, carry):
            for u in range(per):
                i = p * per + u
                rows = pl.ds(pl.multiple_of(i * blk, blk), blk)
                value = merged[c][rows, :] + jnp.concatenate([product(i), product(i + half)], axis=1)
                if final:
                    g, lane = c * w // blk, c * w % blk
                    under = pl.ds(pl.multiple_of(i * blk, blk) + hrows, blk)
                    outb[g, rows, lane:lane + w] = value[:, :w]
                    outb[g, under, lane:lane + w] = value[:, w:]
                else:
                    merged[c][rows, :] = value
                    low[c][i] = value.astype(BF16)
            if l < levels - 1:
                level_copy(s, l + 1, c, p).start()
            return carry

        lax.fori_loop(0, PIECES, piece, 0)

    done = set()
    first_step()
    for s, t, c in plan(levels, col_levels):
        if t == -2:
            gather_stage(s, c)
        elif t == -1:
            interior_stage(s, c)
        else:
            merge_stage(s, t, c)
        if s == STEPS - 1 and t == levels - 1:
            done.add(c)
            g = c * w // blk
            if all(k in done for k in range(CHUNKS) if k * w // blk == g):
                for p in range(PIECES):
                    out_copy(g, p).start()
    for g in range(rhs // blk):
        for p in range(PIECES):
            out_copy(g, p).wait()


def per_device(mesh, voltage, sources, capacity, inverse, couple, boundary, panels, pattern):
    ncol, nrow = mesh.shape["col"], mesh.shape["row"]
    _, _, levels, nb, kb, blk, _ = panels.shape
    ni, rhs = voltage.shape[2:]
    nbnd = boundary.shape[2]
    w = rhs // CHUNKS
    sems = pltpu.SemaphoreType.DMA
    scratch = [
        pltpu.VMEM((ni, ni), BF16),
        pltpu.VMEM((levels, nb, kb, blk, blk), BF16),
        pltpu.VMEM((nbnd, ncol * nbnd), BF16),
        pltpu.VMEM((ni, rhs), BF16),
        pltpu.VMEM((ni, rhs), BF16),
        pltpu.VMEM((ni, blk), F32),
        pltpu.VMEM((ni, nbnd), BF16),
        pltpu.VMEM((nbnd, ni), BF16),
        pltpu.VMEM((rhs // blk, ni, blk), F32),
        pltpu.VMEM((ni, rhs), BF16),
        pltpu.VMEM((ni, w), BF16),
        pltpu.VMEM((nb, blk, w), BF16),
        pltpu.VMEM((ncol, nbnd, rhs), BF16),
        sems((4 + levels,)),
        sems((rhs // blk, PIECES)),
        sems((STEPS, CHUNKS, ncol)),
        sems((STEPS, CHUNKS, ncol)),
        sems((STEPS, levels, CHUNKS, PIECES)),
        sems((STEPS, levels, CHUNKS, PIECES)),
    ]
    scratch += [pltpu.VMEM((ni // 2, blk), F32) for _ in range(CHUNKS)]
    scratch += [pltpu.VMEM((nb // 2, blk, blk), BF16) for _ in range(CHUNKS)]
    scratch += [pltpu.VMEM((ncol, nbnd // 2, 2 * w), BF16) for _ in range((STEPS - 1) * CHUNKS)]
    scratch += [pltpu.VMEM((nb // 2, blk, blk), BF16) for _ in range(STEPS * levels * CHUNKS)]
    vmem = pl.BlockSpec(memory_space=pltpu.VMEM)
    smem = pl.BlockSpec(memory_space=pltpu.SMEM)
    hbm = pl.BlockSpec(memory_space=pl.ANY)
    return pl.pallas_call(
        functools.partial(kernel, ncol, nrow, levels, nb, kb, blk, nbnd, rhs),
        out_shape=jax.ShapeDtypeStruct((1, 1, ni, rhs), F32),
        in_specs=[vmem, vmem, smem, hbm, hbm, hbm, hbm, hbm],
        out_specs=hbm,
        scratch_shapes=scratch,
        compiler_params=pltpu.CompilerParams(
            collective_id=0, has_side_effects=True, vmem_limit_bytes=67_043_328),
    )(capacity.reshape(1, ni), boundary.reshape(1, nbnd), pattern, voltage, sources, inverse, couple, panels)


def solution(mesh):
    return jax.shard_map(
        functools.partial(per_device, mesh),
        mesh=mesh,
        in_specs=(
            P("row", "col", None, None),
            P("row", "col", None, None),
            P("row", "col", None),
            P("row", "col", None, None),
            P("row", "col", None, None),
            P("row", "col", None),
            P("row", "col", None, None, None, None, None),
            P("row", "col", None, None, None),
        ),
        out_specs=P("row", "col", None, None),
        check_vma=False,
    )
```

time: 224 us -> 194 us (0.87)
  Pallas kernels: 220 us -> 190 us
    pallas_call x1, Pallas kernels: 220 us -> 190 us  [per_device(): pl.pallas_call(functools.partial(kernel, ncol, nrow, levels, nb, kb, blk,...]
where the time goes in v2:
time: 194 us
  Pallas kernels  190 us (98%)
  local copies, waits for them, and re-layouts  4.46 us (2%)
    pallas_call x1, Pallas kernels, per_device(): pl.pallas_call(functools.partial(kernel, ncol, nrow, levels, nb, kb, blk,...  190 us
    unnamed x2, local copies, waits for them, and re-layouts  4.46 us

profile of v2, /device:TPU:0, one launch (start us, length us, event | category | flops | bytes accessed | tf_op | source)
XLA Modules:
  0.0 194.1 jit_solution(811822433476623874)
XLA Ops:
  0.0 1.4 copy.9.pat_ref
  1.4 189.6 %shard_map.82 = f32[1,1,2048,256]{3,2,1,0:T(8,128)} custom-call(f32[1,2048]{1,0:T(1,128)} %bitcast.2, s32[1,256]{1,0:T(1,128)} %bitcast.3, s32[1,1,5,16,3]{4,3,2,1,0:T(8,128)} %copy.9.pat_ref, bf16[1,1,2048,256]{3,2,1,0:T(8,128)(2,1)} %volt_hbm.1, bf16[1,1,2048,256]{3,2,1,0:T(8,128)(2,1)} %src_hbm.1, bf16[1,1,2048,2048]{3,2,1,0:T(8,128)(2,1)} %inv_hbm.1, ...), custom_call_target="tpu_custom_call" | custom-call | tf_op jit(solution)/shard_map/pallas_call | solution.py:307
  191.0 3.0 %copy.11 = f32[1,1,2048,256]{3,2,1,0:T(8,128)} copy(f32[1,1,2048,256]{3,2,1,0:T(8,128)} %shard_map.82) | data formatting | bytes 4194304
